TPU v7x, 32 devices: a whole 2x2x4 slice. The times are simulated.
32 devices in a mesh: mem: 8 (over y, x, core), lat: 4 (over z).
Axes of the slice: x: 2, y: 2, z: 4, core: 2. Of those that a mesh axis runs over, the one named last changes fastest.
Arguments:
- coarse_weights: bfloat16 [32, 32, 8, 128], P('lat', 'mem'), may hold values from -6 to 6
- perturbations: bfloat16 [32, 8, 128, 512], P('mem', None, 'lat'), may hold values from -6 to 6
- lat_matrix: bfloat16 [128, 32], P('lat'), may hold values from -1 to 1
- lon_matrix: bfloat16 [128, 512], replicated, may hold values from -0.5 to 0.5
- wind_field: float32 [2, 128, 512], P(None, 'lat', 'mem'), may hold values from -0.4 to 0.4
- observed_cell: int32 [4, 8, 128, 64], P(None, None, 'lat', 'mem'), may hold values from 0 to 7
- observed_value: float32 [4, 8, 128, 64], P(None, None, 'lat', 'mem'), may hold values from -6 to 6
- observed_weight: float32 [4, 8, 128, 64], P(None, None, 'lat', 'mem'), may hold values from 0.5 to 4
Outputs:
- gradient: float32 [32, 32, 8, 128], P('lat', 'mem')
- increment: float32 [8, 128, 512], P(None, 'lat', 'mem')
Inputs may be any that keep to these rules, and one draw needn't show every extreme that they name: `observed_cell`: the observed cell is an offset within its block of 8 longitudes.
All inputs are finite; a program needn't handle non-finite values.
Results may differ from a plain program's by a relative error of at most 0.0003.
Values may be sent and summed in bfloat16 or wider, within the bound.
A program may use at most 64 MiB of HBM per device.

v0:
```python
import jax
import jax.numpy as jnp
from jax import lax
from jax.sharding import PartitionSpec as P

STEPS = 4
OBLK = 8
diffusion = 0.2
highest = lax.Precision.HIGHEST


def padded_2(value, sides, width):
    for axis, dim in sides:
        peers, length = (lax.axis_size(axis), value.shape[dim])
        up = [(i, (i + 1) % peers) for i in range(peers - 1)]
        down = [(j, i) for i, j in up]
        last = lax.slice_in_dim(value, length - width, length, axis=dim)
        initial = lax.slice_in_dim(value, 0, width, axis=dim)
        before = lax.ppermute(last, axis, up)
        after = lax.ppermute(initial, axis, down)
        value = jnp.concatenate([before, value, after], axis=dim)
    return value


def stencil_parts(padded):
    center = padded[:, 1:-1, 1:-1]
    north_cell = padded[:, 2:, 1:-1]
    south_cell = padded[:, :-2, 1:-1]
    east_cell = padded[:, 1:-1, 2:]
    west_cell = padded[:, 1:-1, :-2]
    return (center, north_cell, south_cell, east_cell, west_cell)


def advance(padded, wind_out):
    center, north_cell, south_cell, east_cell, west_cell = stencil_parts(padded)
    spread = north_cell + south_cell + east_cell + west_cell - 4.0 * center
    return (
        center
        + diffusion * spread
        - 0.5 * wind_out[1] * (north_cell - south_cell)
        - 0.5 * wind_out[0] * (east_cell - west_cell)
    )


def retreat(padded, wind_in):
    center, north_cell, south_cell, east_cell, west_cell = stencil_parts(padded)
    spread = north_cell + south_cell + east_cell + west_cell - 4.0 * center
    along_lon = wind_in[0] * padded
    along_lat = wind_in[1] * padded
    return (
        center
        + diffusion * spread
        + 0.5 * (along_lat[:, 2:, 1:-1] - along_lat[:, :-2, 1:-1])
        + 0.5 * (along_lon[:, 1:-1, 2:] - along_lon[:, 1:-1, :-2])
    )


def observe(tangent, picked, observed, weighting):
    levels, row_count, col_count = tangent.shape
    blocks = tangent.reshape(levels, row_count, col_count // OBLK, OBLK)
    onehot = (picked[..., None] == jnp.arange(OBLK, dtype=jnp.int32)).astype(jnp.float32)
    looked = jnp.sum(blocks * onehot, axis=-1)
    misfit = weighting * (looked - observed)
    return (misfit[..., None] * onehot).reshape(levels, row_count, col_count)


def domain_mask(margin, row_count, col_count):
    lat_start = lax.axis_index("lat") * row_count - margin
    lon_start = lax.axis_index("mem") * col_count - margin
    row_place = lat_start + jnp.arange(row_count + 2 * margin, dtype=jnp.int32)
    col_place = lon_start + jnp.arange(col_count + 2 * margin, dtype=jnp.int32)
    rows_inside = (row_place >= 0) & (row_place < row_count * lax.axis_size("lat"))
    cols_inside = (col_place >= 0) & (col_place < col_count * lax.axis_size("mem"))
    return (rows_inside[:, None] & cols_inside[None, :]).astype(jnp.float32)


def body(
    coarse_weights,
    perturbations,
    lat_matrix,
    lon_matrix,
    wind_field,
    observed_cell,
    observed_value,
    observed_weight,
):
    members_here, levels, row_count, lon_total = perturbations.shape
    col_count = wind_field.shape[2]
    members_all = members_here * lax.axis_size("mem")
    member_scale = 1.0 / jnp.sqrt(jnp.float32(members_all - 1))
    lat_full = lat_matrix.astype(jnp.float32)
    lon_full = lon_matrix.astype(jnp.float32)
    widened = jnp.einsum(
        "cmlw,wf->cmlf", coarse_weights.astype(jnp.float32), lon_full, precision=highest
    )
    columns = lat_full
    localized = jnp.einsum(
        "rc,cmlf->mlrf",
        columns,
        lax.all_gather(widened, "lat", axis=0, tiled=True),
        precision=highest,
    )
    partial_sum = jnp.sum(localized * perturbations, axis=0)
    increment = lax.psum_scatter(partial_sum, "mem", scatter_dimension=2, tiled=True) * member_scale
    wide_wind = padded_2(wind_field, (("mem", 2), ("lat", 1)), STEPS)

    def wind_margin(margin):
        return wide_wind[
            :,
            STEPS - margin : STEPS + row_count + margin,
            STEPS - margin : STEPS + col_count + margin,
        ]

    forcings = []
    tangent = padded_2(increment, (("mem", 2), ("lat", 1)), STEPS)
    for step_index in range(STEPS):
        margin = STEPS - step_index - 1
        tangent = advance(tangent, wind_margin(margin)) * domain_mask(margin, row_count, col_count)
        inner = tangent[:, margin : margin + row_count, margin : margin + col_count]
        forcings.append(
            observe(
                inner,
                observed_cell[step_index],
                observed_value[step_index],
                observed_weight[step_index],
            )
        )
    adjoint = jnp.zeros_like(increment)
    for step_index in reversed(range(STEPS)):
        padded = padded_2(adjoint + forcings[step_index], (("mem", 2), ("lat", 1)), 1)
        adjoint = retreat(padded, wind_margin(1))
    product = perturbations * lax.all_gather(adjoint, "mem", axis=2, tiled=True)[None]
    projected = jnp.einsum("mlrf,wf->mlrw", product, lon_full, precision=highest)
    columns = lat_full
    banded = lax.psum_scatter(
        jnp.einsum("rc,mlrw->cmlw", columns, projected, precision=highest),
        "lat",
        scatter_dimension=0,
        tiled=True,
    )
    gradient = banded * member_scale + coarse_weights.astype(jnp.float32)
    return (gradient, increment)


def solution(mesh):
    in_specs = (
        P("lat", "mem", None, None),
        P("mem", None, "lat", None),
        P("lat", None),
        P(),
        P(None, "lat", "mem"),
        P(None, None, "lat", "mem"),
        P(None, None, "lat", "mem"),
        P(None, None, "lat", "mem"),
    )
    out_specs = (P("lat", "mem", None, None), P(None, "lat", "mem"))
    return jax.shard_map(body, mesh=mesh, in_specs=in_specs, out_specs=out_specs, check_vma=False)
```

profile of v0, /device:TPU:0, one launch (start us, length us, event | category | flops | bytes accessed | tf_op | source)
XLA Modules:
  0.0 257.9 jit_solution(16076721269377844049)
XLA Ops:
  8.1 1.9 fusion.53
  11.5 2.4 collective-permute-start.4
  19.0 39.5 %all-gather.2.cloned.1.call-done = f32[32,4,8,512]{3,0,2,1:T(8,128)} async-done(((f32[8,4,8,512]{3,0,2,1:T(8,128)}), f32[32,4,8,512]{3,0,2,1:T(8,128)}) %all-gather.2.cloned.1.call-update) | async-done | bytes 2097168 | tf_op jit(solution)/shard_map/all_gather | solution.py:100
  58.5 3.7 %fusion = f32[8,32,512]{2,1,0:T(8,128)} fusion(bf16[4,8,32,512]{3,2,1,0:T(8,128)(2,1)S(1)} %copy-done.1, f32[32,4,8,512]{3,0,2,1:T(8,128)} %all-gather.2.cloned.1.call-done, bf16[32,32]{1,0:T(8,128)(2,1)} %param.10), kind=kOutput, calls=%fused_computation.2 | convolution fusion | flops 202768384 | bytes 3672064 | tf_op jit(solution)/shard_map/rc,cmlf->mlrf/dot_general | solution.py:97
  62.2 1.8 copy.254
  65.7 2.1 collective-permute-start.6
  69.4 3.9 %collective-permute-done.7 = f32[2,4,72]{2,1,0:T(4,128)S(1)} collective-permute-done((f32[2,4,72]{2,1,0:T(4,128)S(1)}, f32[2,4,72]{2,1,0:T(4,128)S(1)}, u32[]{:S(2)}, u32[]{:S(2)}) %collective-permute-start.7) | collective-permute-done | bytes 2336 | tf_op jit(solution)/shard_map/ppermute | solution.py:20
  74.2 24.3 %reduce-scatter.7.cloned.1.call-done = f32[64,256]{1,0:T(8,128)} async-done(((f32[512,256]{1,0:T(8,128)}), f32[64,256]{1,0:T(8,128)}) %reduce-scatter.7.cloned.1.call-update) | async-done | bytes 65552
  102.5 3.5 %collective-permute-done.1 = f32[8,32,4]{2,1,0:T(8,128)S(1)} collective-permute-done((f32[8,32,4]{2,1,0:T(8,128)S(1)}, f32[8,32,4]{2,1,0:T(8,128)S(1)}, u32[]{:S(2)}, u32[]{:S(2)}) %collective-permute-start.1) | collective-permute-done | bytes 4128 | tf_op jit(solution)/shard_map/ppermute | solution.py:20
  106.3 3.4 %collective-permute-start.2 = (f32[8,4,72]{1,2,0:T(8,128)S(1)}, f32[8,4,72]{1,2,0:T(8,128)S(1)}, u32[]{:S(2)}, u32[]{:S(2)}) collective-permute-start(f32[8,4,72]{1,2,0:T(8,128)S(1)} %copy.233), channel_id=1, source_target_pairs={{0,1},{1,2},{2,3},{4,5},{5,6},{6,7},{8,9},{9,10},{10,11},{12,13},{... | collective-permute-start | bytes 27656 | tf_op jit(solution)/shard_map/ppermute | solution.py:19
  112.1 2.5 collective-permute-done.2
  114.6 4.9 %collective-permute-done.3 = f32[8,4,72]{1,2,0:T(8,128)S(1)} collective-permute-done((f32[8,4,72]{1,2,0:T(8,128)S(1)}, f32[8,4,72]{1,2,0:T(8,128)S(1)}, u32[]{:S(2)}, u32[]{:S(2)}) %collective-permute-start.3) | collective-permute-done | bytes 9248 | tf_op jit(solution)/shard_map/ppermute | solution.py:20
  121.7 4.0 %collective-permute-start.8 = (f32[8,32,1]{1,2,0:T(1,128)S(1)}, f32[8,32,1]{1,2,0:T(1,128)S(1)}, u32[]{:S(2)}, u32[]{:S(2)}) collective-permute-start(f32[8,32,1]{1,2,0:T(1,128)S(1)} %get-tuple-element.40), channel_id=1, source_target_pairs={{0,4},{4,8},{8,12},{12,16},{16,20},{20,24},{24,28},{1,5},{5,9},{9,... | collective-permute-start | bytes 3080 | tf_op jit(solution)/shard_map/ppermute | solution.py:19
  127.1 3.5 %collective-permute-done.9 = f32[8,32,1]{1,2,0:T(1,128)S(1)} collective-permute-done((f32[8,32,1]{1,2,0:T(1,128)S(1)}, f32[8,32,1]{1,2,0:T(1,128)S(1)}, u32[]{:S(2)}, u32[]{:S(2)}) %collective-permute-start.9) | collective-permute-done | bytes 1056 | tf_op jit(solution)/shard_map/ppermute | solution.py:20
  132.1 4.6 %collective-permute-start.11 = (f32[8,1,66]{1,2,0:T(8,128)S(1)}, f32[8,1,66]{1,2,0:T(8,128)S(1)}, u32[]{:S(2)}, u32[]{:S(2)}) collective-permute-start(f32[8,1,66]{1,2,0:T(8,128)S(1)} %get-tuple-element.28), channel_id=1, source_target_pairs={{0,1},{1,2},{2,3},{4,5},{5,6},{6,7},{8,9},{9,10},{10,11},{12,13},{... | collective-permute-start | bytes 6344 | tf_op jit(solution)/shard_map/ppermute | solution.py:19
  136.8 4.3 %collective-permute-done.10 = f32[8,1,66]{1,2,0:T(8,128)S(1)} collective-permute-done((f32[8,1,66]{1,2,0:T(8,128)S(1)}, f32[8,1,66]{1,2,0:T(8,128)S(1)}, u32[]{:S(2)}, u32[]{:S(2)}) %collective-permute-start.10) | collective-permute-done | bytes 2144 | tf_op jit(solution)/shard_map/ppermute | solution.py:20
  141.1 1.7 collective-permute-done.11
  143.7 3.1 %collective-permute-start.12 = (f32[8,32,1]{1,2,0:T(1,128)S(1)}, f32[8,32,1]{1,2,0:T(1,128)S(1)}, u32[]{:S(2)}, u32[]{:S(2)}) collective-permute-start(f32[8,32,1]{1,2,0:T(1,128)S(1)} %get-tuple-element.38), channel_id=1, source_target_pairs={{0,4},{4,8},{8,12},{12,16},{16,20},{20,24},{24,28},{1,5},{5,9},{9,... | collective-permute-start | bytes 3080 | tf_op jit(solution)/shard_map/ppermute | solution.py:19
  148.1 1.8 collective-permute-done.13
  151.4 4.9 %collective-permute-start.15 = (f32[8,1,66]{1,2,0:T(8,128)S(1)}, f32[8,1,66]{1,2,0:T(8,128)S(1)}, u32[]{:S(2)}, u32[]{:S(2)}) collective-permute-start(f32[8,1,66]{1,2,0:T(8,128)S(1)} %get-tuple-element.26), channel_id=1, source_target_pairs={{0,1},{1,2},{2,3},{4,5},{5,6},{6,7},{8,9},{9,10},{10,11},{12,13},{... | collective-permute-start | bytes 6344 | tf_op jit(solution)/shard_map/ppermute | solution.py:19
  156.3 4.1 %collective-permute-done.14 = f32[8,1,66]{1,2,0:T(8,128)S(1)} collective-permute-done((f32[8,1,66]{1,2,0:T(8,128)S(1)}, f32[8,1,66]{1,2,0:T(8,128)S(1)}, u32[]{:S(2)}, u32[]{:S(2)}) %collective-permute-start.14) | collective-permute-done | bytes 2144 | tf_op jit(solution)/shard_map/ppermute | solution.py:20
  162.9 3.5 %collective-permute-start.16 = (f32[8,32,1]{1,2,0:T(1,128)S(1)}, f32[8,32,1]{1,2,0:T(1,128)S(1)}, u32[]{:S(2)}, u32[]{:S(2)}) collective-permute-start(f32[8,32,1]{1,2,0:T(1,128)S(1)} %get-tuple-element.36), channel_id=1, source_target_pairs={{0,4},{4,8},{8,12},{12,16},{16,20},{20,24},{24,28},{1,5},{5,9},{9,... | collective-permute-start | bytes 3080 | tf_op jit(solution)/shard_map/ppermute | solution.py:19
  167.8 1.8 collective-permute-done.17
  171.0 5.0 %collective-permute-start.19 = (f32[8,1,66]{1,2,0:T(8,128)S(1)}, f32[8,1,66]{1,2,0:T(8,128)S(1)}, u32[]{:S(2)}, u32[]{:S(2)}) collective-permute-start(f32[8,1,66]{1,2,0:T(8,128)S(1)} %get-tuple-element.24), channel_id=1, source_target_pairs={{0,1},{1,2},{2,3},{4,5},{5,6},{6,7},{8,9},{9,10},{10,11},{12,13},{... | collective-permute-start | bytes 6344 | tf_op jit(solution)/shard_map/ppermute | solution.py:19
  176.0 4.2 %collective-permute-done.18 = f32[8,1,66]{1,2,0:T(8,128)S(1)} collective-permute-done((f32[8,1,66]{1,2,0:T(8,128)S(1)}, f32[8,1,66]{1,2,0:T(8,128)S(1)}, u32[]{:S(2)}, u32[]{:S(2)}) %collective-permute-start.18) | collective-permute-done | bytes 2144 | tf_op jit(solution)/shard_map/ppermute | solution.py:20
  182.7 3.5 %collective-permute-start.20 = (f32[8,32,1]{1,2,0:T(1,128)S(1)}, f32[8,32,1]{1,2,0:T(1,128)S(1)}, u32[]{:S(2)}, u32[]{:S(2)}) collective-permute-start(f32[8,32,1]{1,2,0:T(1,128)S(1)} %get-tuple-element.30), channel_id=1, source_target_pairs={{0,4},{4,8},{8,12},{12,16},{16,20},{20,24},{24,28},{1,5},{5,9},{9,... | collective-permute-start | bytes 3080 | tf_op jit(solution)/shard_map/ppermute | solution.py:19
  187.5 2.0 collective-permute-done.21
  190.9 5.0 %collective-permute-start.23 = (f32[8,1,66]{1,2,0:T(8,128)S(1)}, f32[8,1,66]{1,2,0:T(8,128)S(1)}, u32[]{:S(2)}, u32[]{:S(2)}) collective-permute-start(f32[8,1,66]{1,2,0:T(8,128)S(1)} %get-tuple-element.22), channel_id=1, source_target_pairs={{0,1},{1,2},{2,3},{4,5},{5,6},{6,7},{8,9},{9,10},{10,11},{12,13},{... | collective-permute-start | bytes 6344 | tf_op jit(solution)/shard_map/ppermute | solution.py:19
  196.0 4.2 %collective-permute-done.22 = f32[8,1,66]{1,2,0:T(8,128)S(1)} collective-permute-done((f32[8,1,66]{1,2,0:T(8,128)S(1)}, f32[8,1,66]{1,2,0:T(8,128)S(1)}, u32[]{:S(2)}, u32[]{:S(2)}) %collective-permute-start.22) | collective-permute-done | bytes 2144 | tf_op jit(solution)/shard_map/ppermute | solution.py:20
  202.7 17.4 %all_gather.7 = f32[8,32,512]{1,2,0:T(8,128)S(1)} all-gather(f32[8,32,64]{1,2,0:T(8,128)S(1)} %fusion.4), channel_id=1, replica_groups=mesh['mem'=8,'lat'=4] {'mem'}, dimensions={2}, use_global_device_ids=true | all-gather | bytes 589824 | tf_op jit(solution)/shard_map/all_gather | solution.py:132
  221.5 2.2 fusion.1
  225.0 24.8 %reduce-scatter.5.cloned.1.call-done = f32[8,4,8,128]{3,0,2,1:T(8,128)} async-done(((f32[32,4,8,128]{3,0,2,1:T(8,128)}), f32[8,4,8,128]{3,0,2,1:T(8,128)}) %reduce-scatter.5.cloned.1.call-update) | async-done | bytes 131088 | tf_op jit(solution)/shard_map/reduce_scatter | solution.py:135
  (130 shorter events, 44.0 us)
Async XLA Ops:
  7.2 51.3 %copy-start.1 = (bf16[4,8,32,512]{3,2,1,0:T(8,128)(2,1)S(1)}, bf16[4,8,32,512]{3,2,1,0:T(8,128)(2,1)}, u32[]{:S(2)}) copy-start(bf16[4,8,32,512]{3,2,1,0:T(8,128)(2,1)} %param.9) | copy-start | bytes 3145732
  7.2 51.3 %all-gather.2.cloned.1.call-start = ((), (), s32[]{:S(2)}) async-start(), calls=%async_computation.2 | async-start | bytes 2621440 | tf_op jit(solution)/shard_map/all_gather | solution.py:100
  10.0 88.6 %reduce-scatter.7.cloned.1.call-start = ((), (), s32[]{:S(2)}) async-start(), calls=%async_computation.4 | async-start | bytes 589824
  11.5 54.0 %collective-permute-start.4 = (f32[2,32,4]{2,1,0:T(8,128)}, f32[2,32,4]{2,1,0:T(8,128)S(1)}, u32[]{:S(2)}, u32[]{:S(2)}) collective-permute-start(f32[2,32,4]{2,1,0:T(8,128)} %get-tuple-element.62), channel_id=1, source_target_pairs={{0,4},{4,8},{8,12},{12,16},{16,20},{20,24},{24,28},{1,5},{5,9},{9,... | collective-permute-start | bytes 3080 | tf_op jit(solution)/shard_map/ppermute | solution.py:19
  13.9 51.6 %collective-permute-start.5 = (f32[2,32,4]{2,1,0:T(8,128)}, f32[2,32,4]{2,1,0:T(8,128)S(1)}, u32[]{:S(2)}, u32[]{:S(2)}) collective-permute-start(f32[2,32,4]{2,1,0:T(8,128)} %get-tuple-element.63), channel_id=1, source_target_pairs={{4,0},{8,4},{12,8},{16,12},{20,16},{24,20},{28,24},{5,1},{9,5},{13... | collective-permute-start | bytes 3080 | tf_op jit(solution)/shard_map/ppermute | solution.py:20
  65.5 184.3 %reduce-scatter.5.cloned.1.call-start = ((), (), s32[]{:S(2)}) async-start(), calls=%async_computation.3 | async-start | bytes 655360 | tf_op jit(solution)/shard_map/reduce_scatter | solution.py:135
  65.7 3.7 %collective-permute-start.6 = (f32[2,4,72]{2,1,0:T(4,128)S(1)}, f32[2,4,72]{2,1,0:T(4,128)S(1)}, u32[]{:S(2)}, u32[]{:S(2)}) collective-permute-start(f32[2,4,72]{2,1,0:T(4,128)S(1)} %get-tuple-element.50), channel_id=1, source_target_pairs={{0,1},{1,2},{2,3},{4,5},{5,6},{6,7},{8,9},{9,10},{10,11},{12,13},{... | collective-permute-start | bytes 6920 | tf_op jit(solution)/shard_map/ppermute | solution.py:19
  67.8 5.5 %collective-permute-start.7 = (f32[2,4,72]{2,1,0:T(4,128)S(1)}, f32[2,4,72]{2,1,0:T(4,128)S(1)}, u32[]{:S(2)}, u32[]{:S(2)}) collective-permute-start(f32[2,4,72]{2,1,0:T(4,128)S(1)} %get-tuple-element.51), channel_id=1, source_target_pairs={{1,0},{2,1},{3,2},{5,4},{6,5},{7,6},{9,8},{10,9},{11,10},{13,12},{... | collective-permute-start | bytes 6920 | tf_op jit(solution)/shard_map/ppermute | solution.py:20
  99.6 20.0 %copy-start.7 = (f32[38,70]{0,1:T(8,128)S(1)}, f32[38,70]{0,1:T(8,128)}, u32[]{:S(2)}) copy-start(f32[38,70]{0,1:T(8,128)} %and_convert_fusion.2) | copy-start | bytes 31924
  99.7 20.4 %copy-start.2 = (f32[8,32,64]{2,1,0:T(8,128)}, f32[8,32,64]{2,1,0:T(8,128)S(1)}, u32[]{:S(2)}) copy-start(f32[8,32,64]{2,1,0:T(8,128)S(1)} %broadcast_multiply_fusion.8) | copy-start | bytes 196612
  99.8 2.7 %collective-permute-start = (f32[8,32,4]{2,1,0:T(8,128)S(1)}, f32[8,32,4]{2,1,0:T(8,128)S(1)}, u32[]{:S(2)}, u32[]{:S(2)}) collective-permute-start(f32[8,32,4]{2,1,0:T(8,128)S(1)} %get-tuple-element.48), channel_id=1, source_target_pairs={{0,4},{4,8},{8,12},{12,16},{16,20},{20,24},{24,28},{1,5},{5,9},{9,... | collective-permute-start | bytes 12296 | tf_op jit(solution)/shard_map/ppermute | solution.py:19
  101.1 4.9 %collective-permute-start.1 = (f32[8,32,4]{2,1,0:T(8,128)S(1)}, f32[8,32,4]{2,1,0:T(8,128)S(1)}, u32[]{:S(2)}, u32[]{:S(2)}) collective-permute-start(f32[8,32,4]{2,1,0:T(8,128)S(1)} %get-tuple-element.49), channel_id=1, source_target_pairs={{4,0},{8,4},{12,8},{16,12},{20,16},{24,20},{28,24},{5,1},{9,5},{13... | collective-permute-start | bytes 12296 | tf_op jit(solution)/shard_map/ppermute | solution.py:20
  106.3 8.2 %collective-permute-start.2 = (f32[8,4,72]{1,2,0:T(8,128)S(1)}, f32[8,4,72]{1,2,0:T(8,128)S(1)}, u32[]{:S(2)}, u32[]{:S(2)}) collective-permute-start(f32[8,4,72]{1,2,0:T(8,128)S(1)} %copy.233), channel_id=1, source_target_pairs={{0,1},{1,2},{2,3},{4,5},{5,6},{6,7},{8,9},{9,10},{10,11},{12,13},{... | collective-permute-start | bytes 27656 | tf_op jit(solution)/shard_map/ppermute | solution.py:19
  109.8 10.3 %copy-start.6 = (f32[36,68]{0,1:T(8,128)S(1)}, f32[36,68]{0,1:T(8,128)}, u32[]{:S(2)}) copy-start(f32[36,68]{0,1:T(8,128)} %and_convert_fusion.1) | copy-start | bytes 29380
  109.9 9.5 %collective-permute-start.3 = (f32[8,4,72]{1,2,0:T(8,128)S(1)}, f32[8,4,72]{1,2,0:T(8,128)S(1)}, u32[]{:S(2)}, u32[]{:S(2)}) collective-permute-start(f32[8,4,72]{1,2,0:T(8,128)S(1)} %copy.234), channel_id=1, source_target_pairs={{1,0},{2,1},{3,2},{5,4},{6,5},{7,6},{9,8},{10,9},{11,10},{13,12},{... | collective-permute-start | bytes 27656 | tf_op jit(solution)/shard_map/ppermute | solution.py:20
  121.7 5.3 %collective-permute-start.8 = (f32[8,32,1]{1,2,0:T(1,128)S(1)}, f32[8,32,1]{1,2,0:T(1,128)S(1)}, u32[]{:S(2)}, u32[]{:S(2)}) collective-permute-start(f32[8,32,1]{1,2,0:T(1,128)S(1)} %get-tuple-element.40), channel_id=1, source_target_pairs={{0,4},{4,8},{8,12},{12,16},{16,20},{20,24},{24,28},{1,5},{5,9},{9,... | collective-permute-start | bytes 3080 | tf_op jit(solution)/shard_map/ppermute | solution.py:19
  125.8 4.8 %collective-permute-start.9 = (f32[8,32,1]{1,2,0:T(1,128)S(1)}, f32[8,32,1]{1,2,0:T(1,128)S(1)}, u32[]{:S(2)}, u32[]{:S(2)}) collective-permute-start(f32[8,32,1]{1,2,0:T(1,128)S(1)} %get-tuple-element.41), channel_id=1, source_target_pairs={{4,0},{8,4},{12,8},{16,12},{20,16},{24,20},{28,24},{5,1},{9,5},{13... | collective-permute-start | bytes 3080 | tf_op jit(solution)/shard_map/ppermute | solution.py:20
  130.8 10.4 %collective-permute-start.10 = (f32[8,1,66]{1,2,0:T(8,128)S(1)}, f32[8,1,66]{1,2,0:T(8,128)S(1)}, u32[]{:S(2)}, u32[]{:S(2)}) collective-permute-start(f32[8,1,66]{1,2,0:T(8,128)S(1)} %get-tuple-element.29), channel_id=1, source_target_pairs={{1,0},{2,1},{3,2},{5,4},{6,5},{7,6},{9,8},{10,9},{11,10},{13,12},{... | collective-permute-start | bytes 6344 | tf_op jit(solution)/shard_map/ppermute | solution.py:20
  132.1 10.8 %collective-permute-start.11 = (f32[8,1,66]{1,2,0:T(8,128)S(1)}, f32[8,1,66]{1,2,0:T(8,128)S(1)}, u32[]{:S(2)}, u32[]{:S(2)}) collective-permute-start(f32[8,1,66]{1,2,0:T(8,128)S(1)} %get-tuple-element.28), channel_id=1, source_target_pairs={{0,1},{1,2},{2,3},{4,5},{5,6},{6,7},{8,9},{9,10},{10,11},{12,13},{... | collective-permute-start | bytes 6344 | tf_op jit(solution)/shard_map/ppermute | solution.py:19
  143.7 4.5 %collective-permute-start.12 = (f32[8,32,1]{1,2,0:T(1,128)S(1)}, f32[8,32,1]{1,2,0:T(1,128)S(1)}, u32[]{:S(2)}, u32[]{:S(2)}) collective-permute-start(f32[8,32,1]{1,2,0:T(1,128)S(1)} %get-tuple-element.38), channel_id=1, source_target_pairs={{0,4},{4,8},{8,12},{12,16},{16,20},{20,24},{24,28},{1,5},{5,9},{9,... | collective-permute-start | bytes 3080 | tf_op jit(solution)/shard_map/ppermute | solution.py:19
  146.8 3.1 %collective-permute-start.13 = (f32[8,32,1]{1,2,0:T(1,128)S(1)}, f32[8,32,1]{1,2,0:T(1,128)S(1)}, u32[]{:S(2)}, u32[]{:S(2)}) collective-permute-start(f32[8,32,1]{1,2,0:T(1,128)S(1)} %get-tuple-element.39), channel_id=1, source_target_pairs={{4,0},{8,4},{12,8},{16,12},{20,16},{24,20},{28,24},{5,1},{9,5},{13... | collective-permute-start | bytes 3080 | tf_op jit(solution)/shard_map/ppermute | solution.py:20
  150.1 10.3 %collective-permute-start.14 = (f32[8,1,66]{1,2,0:T(8,128)S(1)}, f32[8,1,66]{1,2,0:T(8,128)S(1)}, u32[]{:S(2)}, u32[]{:S(2)}) collective-permute-start(f32[8,1,66]{1,2,0:T(8,128)S(1)} %get-tuple-element.27), channel_id=1, source_target_pairs={{1,0},{2,1},{3,2},{5,4},{6,5},{7,6},{9,8},{10,9},{11,10},{13,12},{... | collective-permute-start | bytes 6344 | tf_op jit(solution)/shard_map/ppermute | solution.py:20
  151.4 10.8 %collective-permute-start.15 = (f32[8,1,66]{1,2,0:T(8,128)S(1)}, f32[8,1,66]{1,2,0:T(8,128)S(1)}, u32[]{:S(2)}, u32[]{:S(2)}) collective-permute-start(f32[8,1,66]{1,2,0:T(8,128)S(1)} %get-tuple-element.26), channel_id=1, source_target_pairs={{0,1},{1,2},{2,3},{4,5},{5,6},{6,7},{8,9},{9,10},{10,11},{12,13},{... | collective-permute-start | bytes 6344 | tf_op jit(solution)/shard_map/ppermute | solution.py:19
  162.9 4.8 %collective-permute-start.16 = (f32[8,32,1]{1,2,0:T(1,128)S(1)}, f32[8,32,1]{1,2,0:T(1,128)S(1)}, u32[]{:S(2)}, u32[]{:S(2)}) collective-permute-start(f32[8,32,1]{1,2,0:T(1,128)S(1)} %get-tuple-element.36), channel_id=1, source_target_pairs={{0,4},{4,8},{8,12},{12,16},{16,20},{20,24},{24,28},{1,5},{5,9},{9,... | collective-permute-start | bytes 3080 | tf_op jit(solution)/shard_map/ppermute | solution.py:19
  166.5 3.1 %collective-permute-start.17 = (f32[8,32,1]{1,2,0:T(1,128)S(1)}, f32[8,32,1]{1,2,0:T(1,128)S(1)}, u32[]{:S(2)}, u32[]{:S(2)}) collective-permute-start(f32[8,32,1]{1,2,0:T(1,128)S(1)} %get-tuple-element.37), channel_id=1, source_target_pairs={{4,0},{8,4},{12,8},{16,12},{20,16},{24,20},{28,24},{5,1},{9,5},{13... | collective-permute-start | bytes 3080 | tf_op jit(solution)/shard_map/ppermute | solution.py:20
  169.7 10.4 %collective-permute-start.18 = (f32[8,1,66]{1,2,0:T(8,128)S(1)}, f32[8,1,66]{1,2,0:T(8,128)S(1)}, u32[]{:S(2)}, u32[]{:S(2)}) collective-permute-start(f32[8,1,66]{1,2,0:T(8,128)S(1)} %get-tuple-element.25), channel_id=1, source_target_pairs={{1,0},{2,1},{3,2},{5,4},{6,5},{7,6},{9,8},{10,9},{11,10},{13,12},{... | collective-permute-start | bytes 6344 | tf_op jit(solution)/shard_map/ppermute | solution.py:20
  171.0 10.9 %collective-permute-start.19 = (f32[8,1,66]{1,2,0:T(8,128)S(1)}, f32[8,1,66]{1,2,0:T(8,128)S(1)}, u32[]{:S(2)}, u32[]{:S(2)}) collective-permute-start(f32[8,1,66]{1,2,0:T(8,128)S(1)} %get-tuple-element.24), channel_id=1, source_target_pairs={{0,1},{1,2},{2,3},{4,5},{5,6},{6,7},{8,9},{9,10},{10,11},{12,13},{... | collective-permute-start | bytes 6344 | tf_op jit(solution)/shard_map/ppermute | solution.py:19
  182.7 4.8 %collective-permute-start.20 = (f32[8,32,1]{1,2,0:T(1,128)S(1)}, f32[8,32,1]{1,2,0:T(1,128)S(1)}, u32[]{:S(2)}, u32[]{:S(2)}) collective-permute-start(f32[8,32,1]{1,2,0:T(1,128)S(1)} %get-tuple-element.30), channel_id=1, source_target_pairs={{0,4},{4,8},{8,12},{12,16},{16,20},{20,24},{24,28},{1,5},{5,9},{9,... | collective-permute-start | bytes 3080 | tf_op jit(solution)/shard_map/ppermute | solution.py:19
  186.2 3.3 %collective-permute-start.21 = (f32[8,32,1]{1,2,0:T(1,128)S(1)}, f32[8,32,1]{1,2,0:T(1,128)S(1)}, u32[]{:S(2)}, u32[]{:S(2)}) collective-permute-start(f32[8,32,1]{1,2,0:T(1,128)S(1)} %get-tuple-element.31), channel_id=1, source_target_pairs={{4,0},{8,4},{12,8},{16,12},{20,16},{24,20},{28,24},{5,1},{9,5},{13... | collective-permute-start | bytes 3080 | tf_op jit(solution)/shard_map/ppermute | solution.py:20
  189.6 10.6 %collective-permute-start.22 = (f32[8,1,66]{1,2,0:T(8,128)S(1)}, f32[8,1,66]{1,2,0:T(8,128)S(1)}, u32[]{:S(2)}, u32[]{:S(2)}) collective-permute-start(f32[8,1,66]{1,2,0:T(8,128)S(1)} %get-tuple-element.23), channel_id=1, source_target_pairs={{1,0},{2,1},{3,2},{5,4},{6,5},{7,6},{9,8},{10,9},{11,10},{13,12},{... | collective-permute-start | bytes 6344 | tf_op jit(solution)/shard_map/ppermute | solution.py:20
  190.9 11.0 %collective-permute-start.23 = (f32[8,1,66]{1,2,0:T(8,128)S(1)}, f32[8,1,66]{1,2,0:T(8,128)S(1)}, u32[]{:S(2)}, u32[]{:S(2)}) collective-permute-start(f32[8,1,66]{1,2,0:T(8,128)S(1)} %get-tuple-element.22), channel_id=1, source_target_pairs={{0,1},{1,2},{2,3},{4,5},{5,6},{6,7},{8,9},{9,10},{10,11},{12,13},{... | collective-permute-start | bytes 6344 | tf_op jit(solution)/shard_map/ppermute | solution.py:19
  221.5 28.3 %copy-start.4 = (bf16[8,4,8,128]{3,2,1,0:T(8,128)(2,1)S(1)}, bf16[8,4,8,128]{3,2,1,0:T(8,128)(2,1)}, u32[]{:S(2)}) copy-start(bf16[8,4,8,128]{3,2,1,0:T(8,128)(2,1)} %param.8) | copy-start | bytes 196612
  (8 other events, 15.1 us)
Sparse Core Ops, SparseCore 0:
  10.1 48.3 all-gather.1
  65.6 32.8 reduce-scatter.6
  225.1 24.6 reduce-scatter.4
where the time goes:
time: 259 us; the launch traced here: 258 us
  waiting for transfers between devices  136 us (53%)
  starting transfers between devices  58.4 us (23%)
  blocking collectives  17.4 us (7%)
  between operations  14.5 us (6%)
  local copies, waits for them, and re-layouts  11.8 us (5%)
  other arithmetic  10.6 us (4%)
  matrix products  9.04 us (3%)
    ppermute x12, starting transfers between devices, padded_2(): before = lax.ppermute(last, axis, up)  42.8 us
    all_gather x1, waiting for transfers between devices, body(): lax.all_gather(widened, 'lat', axis=0, tiled=True)  39.5 us
    ppermute x12, waiting for transfers between devices, padded_2(): after = lax.ppermute(initial, axis, down)  38.1 us
    reduce_scatter x1, waiting for transfers between devices, body(): lax.psum_scatter(jnp.einsum('rc,mlrw->cmlw', columns, projected, precisio...  24.8 us
    unnamed x4, waiting for transfers between devices  24.4 us
    all_gather x1, blocking collectives, body(): lax.all_gather(adjoint, 'mem', axis=2, tiled=True)[None]  17.4 us
    ppermute x12, starting transfers between devices, padded_2(): after = lax.ppermute(initial, axis, down)  15.5 us
    ppermute x12, waiting for transfers between devices, padded_2(): before = lax.ppermute(last, axis, up)  9.46 us
  transfers between devices with their start and end apart: 27, of which 19 were waited for; matrix products, arithmetic and copies ran while one was open for 6% of the time, Pallas kernels for 0%

commit v1 on v0

--- a/solution.py
+++ b/solution.py
@@ -7,6 +7,11 @@
 OBLK = 8
 diffusion = 0.2
 highest = lax.Precision.HIGHEST
+
+
+def gather_by_exchange(array, axis, dim):
+    copies = jnp.concatenate([array] * lax.axis_size(axis), axis=dim)
+    return lax.all_to_all(copies, axis, dim, dim, tiled=True)
 
 
 def padded_2(value, sides, width):
@@ -95,10 +100,7 @@
     )
     columns = lat_full
     localized = jnp.einsum(
-        "rc,cmlf->mlrf",
-        columns,
-        lax.all_gather(widened, "lat", axis=0, tiled=True),
-        precision=highest,
+        "rc,cmlf->mlrf", columns, gather_by_exchange(widened, "lat", 0), precision=highest
     )
     partial_sum = jnp.sum(localized * perturbations, axis=0)
     increment = lax.psum_scatter(partial_sum, "mem", scatter_dimension=2, tiled=True) * member_scale

time: 259 us -> 267 us (1.031)
  starting transfers between devices: 58.4 us -> 63.2 us
  waiting for transfers between devices: 136 us -> 140 us
    all_to_all x0 -> x1, waiting for transfers between devices: none -> 41.7 us  [gather_by_exchange(): return lax.all_to_all(copies, axis, dim, dim, tiled=True)]
    all_gather x1 -> x0, waiting for transfers between devices: 39.5 us -> none  [body(): lax.all_gather(widened, 'lat', axis=0, tiled=True)]
    all_to_all x0 -> x1, starting transfers between devices: none -> 6.48 us  [gather_by_exchange(): return lax.all_to_all(copies, axis, dim, dim, tiled=True)]
    unnamed x4 -> x3, waiting for transfers between devices: 24.4 us -> 26.3 us
    unnamed x31 -> x27, local copies, waits for them, and re-layouts: 5.89 us -> 5.93 us
  transfers between devices with their start and end apart: 27 -> 27, of which waited for: 19 -> 19; matrix products, arithmetic and copies ran while one was open for 6% -> 5% of each run, Pallas kernels for 0% -> 0%
where the time goes in v1:
time: 267 us; the launch traced here: 266 us
  waiting for transfers between devices  140 us (52%)
  starting transfers between devices  63.2 us (24%)
  blocking collectives  17.2 us (6%)
  between operations  14.7 us (6%)
  local copies, waits for them, and re-layouts  13.6 us (5%)
  other arithmetic  9.33 us (3%)
  matrix products  7.93 us (3%)
    all_to_all x1, waiting for transfers between devices, gather_by_exchange(): return lax.all_to_all(copies, axis, dim, dim, tiled=True)  41.7 us
    ppermute x12, starting transfers between devices, padded_2(): before = lax.ppermute(last, axis, up)  41.2 us
    ppermute x12, waiting for transfers between devices, padded_2(): after = lax.ppermute(initial, axis, down)  37.9 us
    unnamed x3, waiting for transfers between devices  26.3 us
    reduce_scatter x1, waiting for transfers between devices, body(): lax.psum_scatter(jnp.einsum('rc,mlrw->cmlw', columns, projected, precisio...  24.7 us
    all_gather x1, blocking collectives, body(): lax.all_gather(adjoint, 'mem', axis=2, tiled=True)[None]  17.2 us
    ppermute x12, starting transfers between devices, padded_2(): after = lax.ppermute(initial, axis, down)  15.5 us
    ppermute x12, waiting for transfers between devices, padded_2(): before = lax.ppermute(last, axis, up)  9.46 us
  transfers between devices with their start and end apart: 27, of which 19 were waited for; matrix products, arithmetic and copies ran while one was open for 5% of the time, Pallas kernels for 0%

profile of v1, /device:TPU:0, one launch (start us, length us, event | category | flops | bytes accessed | tf_op | source)
XLA Modules:
  0.0 266.2 jit_solution(16705029233673162082)
XLA Ops:
  9.4 2.6 copy.237
  12.0 6.5 %all-to-all-start = ((f32[32,4,8,512]{3,2,1,0:T(8,128)}), f32[32,4,8,512]{3,2,1,0:T(8,128)S(1)}, u32[]{:S(2)}, u32[]{:S(2)}) async-start(f32[32,4,8,512]{3,2,1,0:T(8,128)} %copy.237), calls=%async_computation | async-start | bytes 4194304 | tf_op jit(solution)/shard_map/all_to_all | solution.py:14
  24.9 41.7 %all-to-all-done = f32[32,4,8,512]{3,2,1,0:T(8,128)S(1)} async-done(((f32[32,4,8,512]{3,2,1,0:T(8,128)}), f32[32,4,8,512]{3,2,1,0:T(8,128)S(1)}, u32[]{:S(2)}, u32[]{:S(2)}) %all-to-all-start) | async-done | bytes 2097184 | tf_op jit(solution)/shard_map/all_to_all | solution.py:14
  66.6 3.4 %fusion = f32[8,32,512]{2,1,0:T(8,128)} fusion(bf16[4,8,32,512]{3,2,1,0:T(8,128)(2,1)S(1)} %copy-done.1, f32[32,4,8,512]{3,2,1,0:T(8,128)S(1)} %all-to-all-done, bf16[32,32]{1,0:T(8,128)(2,1)S(1)} %copy-done.10), kind=kOutput, calls=%fused_computation.2 | convolution fusion | flops 202768384 | bytes 3672064 | tf_op jit(solution)/shard_map/rc,cmlf->mlrf/dot_general | solution.py:102
  70.1 1.8 copy.260
  76.4 3.9 %collective-permute-done.7 = f32[2,4,72]{2,1,0:T(4,128)S(1)} collective-permute-done((f32[2,4,72]{2,1,0:T(4,128)S(1)}, f32[2,4,72]{2,1,0:T(4,128)S(1)}, u32[]{:S(2)}, u32[]{:S(2)}) %collective-permute-start.7) | collective-permute-done | bytes 2336 | tf_op jit(solution)/shard_map/ppermute | solution.py:25
  80.4 26.3 %reduce-scatter.7.cloned.1.call-done = f32[64,256]{1,0:T(8,128)} async-done(((f32[512,256]{1,0:T(8,128)}), f32[64,256]{1,0:T(8,128)}) %reduce-scatter.7.cloned.1.call-update) | async-done | bytes 65552
  110.6 3.5 %collective-permute-done.1 = f32[8,32,4]{2,1,0:T(8,128)S(1)} collective-permute-done((f32[8,32,4]{2,1,0:T(8,128)S(1)}, f32[8,32,4]{2,1,0:T(8,128)S(1)}, u32[]{:S(2)}, u32[]{:S(2)}) %collective-permute-start.1) | collective-permute-done | bytes 4128 | tf_op jit(solution)/shard_map/ppermute | solution.py:25
  114.5 3.4 %collective-permute-start.2 = (f32[8,4,72]{1,2,0:T(8,128)S(1)}, f32[8,4,72]{1,2,0:T(8,128)S(1)}, u32[]{:S(2)}, u32[]{:S(2)}) collective-permute-start(f32[8,4,72]{1,2,0:T(8,128)S(1)} %copy.239), channel_id=1, source_target_pairs={{0,1},{1,2},{2,3},{4,5},{5,6},{6,7},{8,9},{9,10},{10,11},{12,13},{... | collective-permute-start | bytes 27656 | tf_op jit(solution)/shard_map/ppermute | solution.py:24
  120.2 2.5 collective-permute-done.2
  122.7 4.9 %collective-permute-done.3 = f32[8,4,72]{1,2,0:T(8,128)S(1)} collective-permute-done((f32[8,4,72]{1,2,0:T(8,128)S(1)}, f32[8,4,72]{1,2,0:T(8,128)S(1)}, u32[]{:S(2)}, u32[]{:S(2)}) %collective-permute-start.3) | collective-permute-done | bytes 9248 | tf_op jit(solution)/shard_map/ppermute | solution.py:25
  129.9 4.0 %collective-permute-start.8 = (f32[8,32,1]{1,2,0:T(1,128)S(1)}, f32[8,32,1]{1,2,0:T(1,128)S(1)}, u32[]{:S(2)}, u32[]{:S(2)}) collective-permute-start(f32[8,32,1]{1,2,0:T(1,128)S(1)} %get-tuple-element.40), channel_id=1, source_target_pairs={{0,4},{4,8},{8,12},{12,16},{16,20},{20,24},{24,28},{1,5},{5,9},{9,... | collective-permute-start | bytes 3080 | tf_op jit(solution)/shard_map/ppermute | solution.py:24
  135.2 3.5 %collective-permute-done.9 = f32[8,32,1]{1,2,0:T(1,128)S(1)} collective-permute-done((f32[8,32,1]{1,2,0:T(1,128)S(1)}, f32[8,32,1]{1,2,0:T(1,128)S(1)}, u32[]{:S(2)}, u32[]{:S(2)}) %collective-permute-start.9) | collective-permute-done | bytes 1056 | tf_op jit(solution)/shard_map/ppermute | solution.py:25
  140.2 4.6 %collective-permute-start.11 = (f32[8,1,66]{1,2,0:T(8,128)S(1)}, f32[8,1,66]{1,2,0:T(8,128)S(1)}, u32[]{:S(2)}, u32[]{:S(2)}) collective-permute-start(f32[8,1,66]{1,2,0:T(8,128)S(1)} %get-tuple-element.28), channel_id=1, source_target_pairs={{0,1},{1,2},{2,3},{4,5},{5,6},{6,7},{8,9},{9,10},{10,11},{12,13},{... | collective-permute-start | bytes 6344 | tf_op jit(solution)/shard_map/ppermute | solution.py:24
  145.0 4.3 %collective-permute-done.10 = f32[8,1,66]{1,2,0:T(8,128)S(1)} collective-permute-done((f32[8,1,66]{1,2,0:T(8,128)S(1)}, f32[8,1,66]{1,2,0:T(8,128)S(1)}, u32[]{:S(2)}, u32[]{:S(2)}) %collective-permute-start.10) | collective-permute-done | bytes 2144 | tf_op jit(solution)/shard_map/ppermute | solution.py:25
  149.3 1.7 collective-permute-done.11
  151.9 3.1 %collective-permute-start.12 = (f32[8,32,1]{1,2,0:T(1,128)S(1)}, f32[8,32,1]{1,2,0:T(1,128)S(1)}, u32[]{:S(2)}, u32[]{:S(2)}) collective-permute-start(f32[8,32,1]{1,2,0:T(1,128)S(1)} %get-tuple-element.38), channel_id=1, source_target_pairs={{0,4},{4,8},{8,12},{12,16},{16,20},{20,24},{24,28},{1,5},{5,9},{9,... | collective-permute-start | bytes 3080 | tf_op jit(solution)/shard_map/ppermute | solution.py:24
  156.3 1.8 collective-permute-done.13
  159.6 5.0 %collective-permute-start.15 = (f32[8,1,66]{1,2,0:T(8,128)S(1)}, f32[8,1,66]{1,2,0:T(8,128)S(1)}, u32[]{:S(2)}, u32[]{:S(2)}) collective-permute-start(f32[8,1,66]{1,2,0:T(8,128)S(1)} %get-tuple-element.26), channel_id=1, source_target_pairs={{0,1},{1,2},{2,3},{4,5},{5,6},{6,7},{8,9},{9,10},{10,11},{12,13},{... | collective-permute-start | bytes 6344 | tf_op jit(solution)/shard_map/ppermute | solution.py:24
  164.6 3.9 %collective-permute-done.14 = f32[8,1,66]{1,2,0:T(8,128)S(1)} collective-permute-done((f32[8,1,66]{1,2,0:T(8,128)S(1)}, f32[8,1,66]{1,2,0:T(8,128)S(1)}, u32[]{:S(2)}, u32[]{:S(2)}) %collective-permute-start.14) | collective-permute-done | bytes 2144 | tf_op jit(solution)/shard_map/ppermute | solution.py:25
  168.6 1.7 collective-permute-done.15
  171.1 3.5 %collective-permute-start.16 = (f32[8,32,1]{1,2,0:T(1,128)S(1)}, f32[8,32,1]{1,2,0:T(1,128)S(1)}, u32[]{:S(2)}, u32[]{:S(2)}) collective-permute-start(f32[8,32,1]{1,2,0:T(1,128)S(1)} %get-tuple-element.36), channel_id=1, source_target_pairs={{0,4},{4,8},{8,12},{12,16},{16,20},{20,24},{24,28},{1,5},{5,9},{9,... | collective-permute-start | bytes 3080 | tf_op jit(solution)/shard_map/ppermute | solution.py:24
  175.9 1.8 collective-permute-done.17
  179.2 5.0 %collective-permute-start.19 = (f32[8,1,66]{1,2,0:T(8,128)S(1)}, f32[8,1,66]{1,2,0:T(8,128)S(1)}, u32[]{:S(2)}, u32[]{:S(2)}) collective-permute-start(f32[8,1,66]{1,2,0:T(8,128)S(1)} %get-tuple-element.24), channel_id=1, source_target_pairs={{0,1},{1,2},{2,3},{4,5},{5,6},{6,7},{8,9},{9,10},{10,11},{12,13},{... | collective-permute-start | bytes 6344 | tf_op jit(solution)/shard_map/ppermute | solution.py:24
  184.1 4.2 %collective-permute-done.18 = f32[8,1,66]{1,2,0:T(8,128)S(1)} collective-permute-done((f32[8,1,66]{1,2,0:T(8,128)S(1)}, f32[8,1,66]{1,2,0:T(8,128)S(1)}, u32[]{:S(2)}, u32[]{:S(2)}) %collective-permute-start.18) | collective-permute-done | bytes 2144 | tf_op jit(solution)/shard_map/ppermute | solution.py:25
  190.8 3.5 %collective-permute-start.20 = (f32[8,32,1]{1,2,0:T(1,128)S(1)}, f32[8,32,1]{1,2,0:T(1,128)S(1)}, u32[]{:S(2)}, u32[]{:S(2)}) collective-permute-start(f32[8,32,1]{1,2,0:T(1,128)S(1)} %get-tuple-element.30), channel_id=1, source_target_pairs={{0,4},{4,8},{8,12},{12,16},{16,20},{20,24},{24,28},{1,5},{5,9},{9,... | collective-permute-start | bytes 3080 | tf_op jit(solution)/shard_map/ppermute | solution.py:24
  195.6 2.0 collective-permute-done.21
  199.1 5.0 %collective-permute-start.23 = (f32[8,1,66]{1,2,0:T(8,128)S(1)}, f32[8,1,66]{1,2,0:T(8,128)S(1)}, u32[]{:S(2)}, u32[]{:S(2)}) collective-permute-start(f32[8,1,66]{1,2,0:T(8,128)S(1)} %get-tuple-element.22), channel_id=1, source_target_pairs={{0,1},{1,2},{2,3},{4,5},{5,6},{6,7},{8,9},{9,10},{10,11},{12,13},{... | collective-permute-start | bytes 6344 | tf_op jit(solution)/shard_map/ppermute | solution.py:24
  204.1 4.2 %collective-permute-done.22 = f32[8,1,66]{1,2,0:T(8,128)S(1)} collective-permute-done((f32[8,1,66]{1,2,0:T(8,128)S(1)}, f32[8,1,66]{1,2,0:T(8,128)S(1)}, u32[]{:S(2)}, u32[]{:S(2)}) %collective-permute-start.22) | collective-permute-done | bytes 2144 | tf_op jit(solution)/shard_map/ppermute | solution.py:25
  210.8 17.2 %all_gather.3 = f32[8,32,512]{1,2,0:T(8,128)S(1)} all-gather(f32[8,32,64]{1,2,0:T(8,128)S(1)} %fusion.8), channel_id=1, replica_groups=mesh['mem'=8,'lat'=4] {'mem'}, dimensions={2}, use_global_device_ids=true | all-gather | bytes 589824 | tf_op jit(solution)/shard_map/all_gather | solution.py:134
  229.5 2.2 fusion.1
  232.9 24.7 %reduce-scatter.5.cloned.1.call-done = f32[8,4,8,128]{3,0,2,1:T(8,128)} async-done(((f32[32,4,8,128]{3,0,2,1:T(8,128)}), f32[8,4,8,128]{3,0,2,1:T(8,128)}) %reduce-scatter.5.cloned.1.call-update) | async-done | bytes 131088 | tf_op jit(solution)/shard_map/reduce_scatter | solution.py:137
  (127 shorter events, 43.9 us)
Async XLA Ops:
  12.0 54.7 %copy-start.1 = (bf16[4,8,32,512]{3,2,1,0:T(8,128)(2,1)S(1)}, bf16[4,8,32,512]{3,2,1,0:T(8,128)(2,1)}, u32[]{:S(2)}) copy-start(bf16[4,8,32,512]{3,2,1,0:T(8,128)(2,1)} %param.9) | copy-start | bytes 3145732
  12.0 54.7 %copy-start.10 = (bf16[32,32]{1,0:T(8,128)(2,1)S(1)}, bf16[32,32]{1,0:T(8,128)(2,1)}, u32[]{:S(2)}) copy-start(bf16[32,32]{1,0:T(8,128)(2,1)} %param.10) | copy-start | bytes 6148
  12.0 54.7 %all-to-all-start = ((f32[32,4,8,512]{3,2,1,0:T(8,128)}), f32[32,4,8,512]{3,2,1,0:T(8,128)S(1)}, u32[]{:S(2)}, u32[]{:S(2)}) async-start(f32[32,4,8,512]{3,2,1,0:T(8,128)} %copy.237), calls=%async_computation | async-start | bytes 4194304 | tf_op jit(solution)/shard_map/all_to_all | solution.py:14
  18.4 88.3 %reduce-scatter.7.cloned.1.call-start = ((), (), s32[]{:S(2)}) async-start(), calls=%async_computation.4 | async-start | bytes 589824
  19.1 54.2 %collective-permute-start.4 = (f32[2,32,4]{2,1,0:T(8,128)}, f32[2,32,4]{2,1,0:T(8,128)S(1)}, u32[]{:S(2)}, u32[]{:S(2)}) collective-permute-start(f32[2,32,4]{2,1,0:T(8,128)} %get-tuple-element.62), channel_id=1, source_target_pairs={{0,4},{4,8},{8,12},{12,16},{16,20},{20,24},{24,28},{1,5},{5,9},{9,... | collective-permute-start | bytes 3080 | tf_op jit(solution)/shard_map/ppermute | solution.py:24
  20.6 52.8 %collective-permute-start.5 = (f32[2,32,4]{2,1,0:T(8,128)}, f32[2,32,4]{2,1,0:T(8,128)S(1)}, u32[]{:S(2)}, u32[]{:S(2)}) collective-permute-start(f32[2,32,4]{2,1,0:T(8,128)} %get-tuple-element.63), channel_id=1, source_target_pairs={{4,0},{8,4},{12,8},{16,12},{20,16},{24,20},{28,24},{5,1},{9,5},{13... | collective-permute-start | bytes 3080 | tf_op jit(solution)/shard_map/ppermute | solution.py:25
  73.3 184.4 %reduce-scatter.5.cloned.1.call-start = ((), (), s32[]{:S(2)}) async-start(), calls=%async_computation.3 | async-start | bytes 655360 | tf_op jit(solution)/shard_map/reduce_scatter | solution.py:137
  73.5 2.9 %collective-permute-start.6 = (f32[2,4,72]{2,1,0:T(4,128)S(1)}, f32[2,4,72]{2,1,0:T(4,128)S(1)}, u32[]{:S(2)}, u32[]{:S(2)}) collective-permute-start(f32[2,4,72]{2,1,0:T(4,128)S(1)} %get-tuple-element.50), channel_id=1, source_target_pairs={{0,1},{1,2},{2,3},{4,5},{5,6},{6,7},{8,9},{9,10},{10,11},{12,13},{... | collective-permute-start | bytes 6920 | tf_op jit(solution)/shard_map/ppermute | solution.py:24
  74.8 5.5 %collective-permute-start.7 = (f32[2,4,72]{2,1,0:T(4,128)S(1)}, f32[2,4,72]{2,1,0:T(4,128)S(1)}, u32[]{:S(2)}, u32[]{:S(2)}) collective-permute-start(f32[2,4,72]{2,1,0:T(4,128)S(1)} %get-tuple-element.51), channel_id=1, source_target_pairs={{1,0},{2,1},{3,2},{5,4},{6,5},{7,6},{9,8},{10,9},{11,10},{13,12},{... | collective-permute-start | bytes 6920 | tf_op jit(solution)/shard_map/ppermute | solution.py:25
  107.8 20.0 %copy-start.7 = (f32[38,70]{0,1:T(8,128)S(1)}, f32[38,70]{0,1:T(8,128)}, u32[]{:S(2)}) copy-start(f32[38,70]{0,1:T(8,128)} %and_convert_fusion.2) | copy-start | bytes 31924
  107.8 20.4 %copy-start.2 = (f32[8,32,64]{2,1,0:T(8,128)}, f32[8,32,64]{2,1,0:T(8,128)S(1)}, u32[]{:S(2)}) copy-start(f32[8,32,64]{2,1,0:T(8,128)S(1)} %broadcast_multiply_fusion.8) | copy-start | bytes 196612
  107.9 2.7 %collective-permute-start = (f32[8,32,4]{2,1,0:T(8,128)S(1)}, f32[8,32,4]{2,1,0:T(8,128)S(1)}, u32[]{:S(2)}, u32[]{:S(2)}) collective-permute-start(f32[8,32,4]{2,1,0:T(8,128)S(1)} %get-tuple-element.48), channel_id=1, source_target_pairs={{0,4},{4,8},{8,12},{12,16},{16,20},{20,24},{24,28},{1,5},{5,9},{9,... | collective-permute-start | bytes 12296 | tf_op jit(solution)/shard_map/ppermute | solution.py:24
  109.2 4.9 %collective-permute-start.1 = (f32[8,32,4]{2,1,0:T(8,128)S(1)}, f32[8,32,4]{2,1,0:T(8,128)S(1)}, u32[]{:S(2)}, u32[]{:S(2)}) collective-permute-start(f32[8,32,4]{2,1,0:T(8,128)S(1)} %get-tuple-element.49), channel_id=1, source_target_pairs={{4,0},{8,4},{12,8},{16,12},{20,16},{24,20},{28,24},{5,1},{9,5},{13... | collective-permute-start | bytes 12296 | tf_op jit(solution)/shard_map/ppermute | solution.py:25
  114.5 8.2 %collective-permute-start.2 = (f32[8,4,72]{1,2,0:T(8,128)S(1)}, f32[8,4,72]{1,2,0:T(8,128)S(1)}, u32[]{:S(2)}, u32[]{:S(2)}) collective-permute-start(f32[8,4,72]{1,2,0:T(8,128)S(1)} %copy.239), channel_id=1, source_target_pairs={{0,1},{1,2},{2,3},{4,5},{5,6},{6,7},{8,9},{9,10},{10,11},{12,13},{... | collective-permute-start | bytes 27656 | tf_op jit(solution)/shard_map/ppermute | solution.py:24
  118.1 9.5 %collective-permute-start.3 = (f32[8,4,72]{1,2,0:T(8,128)S(1)}, f32[8,4,72]{1,2,0:T(8,128)S(1)}, u32[]{:S(2)}, u32[]{:S(2)}) collective-permute-start(f32[8,4,72]{1,2,0:T(8,128)S(1)} %copy.240), channel_id=1, source_target_pairs={{1,0},{2,1},{3,2},{5,4},{6,5},{7,6},{9,8},{10,9},{11,10},{13,12},{... | collective-permute-start | bytes 27656 | tf_op jit(solution)/shard_map/ppermute | solution.py:25
  129.9 5.3 %collective-permute-start.8 = (f32[8,32,1]{1,2,0:T(1,128)S(1)}, f32[8,32,1]{1,2,0:T(1,128)S(1)}, u32[]{:S(2)}, u32[]{:S(2)}) collective-permute-start(f32[8,32,1]{1,2,0:T(1,128)S(1)} %get-tuple-element.40), channel_id=1, source_target_pairs={{0,4},{4,8},{8,12},{12,16},{16,20},{20,24},{24,28},{1,5},{5,9},{9,... | collective-permute-start | bytes 3080 | tf_op jit(solution)/shard_map/ppermute | solution.py:24
  133.9 4.8 %collective-permute-start.9 = (f32[8,32,1]{1,2,0:T(1,128)S(1)}, f32[8,32,1]{1,2,0:T(1,128)S(1)}, u32[]{:S(2)}, u32[]{:S(2)}) collective-permute-start(f32[8,32,1]{1,2,0:T(1,128)S(1)} %get-tuple-element.41), channel_id=1, source_target_pairs={{4,0},{8,4},{12,8},{16,12},{20,16},{24,20},{28,24},{5,1},{9,5},{13... | collective-permute-start | bytes 3080 | tf_op jit(solution)/shard_map/ppermute | solution.py:25
  138.9 10.4 %collective-permute-start.10 = (f32[8,1,66]{1,2,0:T(8,128)S(1)}, f32[8,1,66]{1,2,0:T(8,128)S(1)}, u32[]{:S(2)}, u32[]{:S(2)}) collective-permute-start(f32[8,1,66]{1,2,0:T(8,128)S(1)} %get-tuple-element.29), channel_id=1, source_target_pairs={{1,0},{2,1},{3,2},{5,4},{6,5},{7,6},{9,8},{10,9},{11,10},{13,12},{... | collective-permute-start | bytes 6344 | tf_op jit(solution)/shard_map/ppermute | solution.py:25
  140.2 10.8 %collective-permute-start.11 = (f32[8,1,66]{1,2,0:T(8,128)S(1)}, f32[8,1,66]{1,2,0:T(8,128)S(1)}, u32[]{:S(2)}, u32[]{:S(2)}) collective-permute-start(f32[8,1,66]{1,2,0:T(8,128)S(1)} %get-tuple-element.28), channel_id=1, source_target_pairs={{0,1},{1,2},{2,3},{4,5},{5,6},{6,7},{8,9},{9,10},{10,11},{12,13},{... | collective-permute-start | bytes 6344 | tf_op jit(solution)/shard_map/ppermute | solution.py:24
  151.9 4.5 %collective-permute-start.12 = (f32[8,32,1]{1,2,0:T(1,128)S(1)}, f32[8,32,1]{1,2,0:T(1,128)S(1)}, u32[]{:S(2)}, u32[]{:S(2)}) collective-permute-start(f32[8,32,1]{1,2,0:T(1,128)S(1)} %get-tuple-element.38), channel_id=1, source_target_pairs={{0,4},{4,8},{8,12},{12,16},{16,20},{20,24},{24,28},{1,5},{5,9},{9,... | collective-permute-start | bytes 3080 | tf_op jit(solution)/shard_map/ppermute | solution.py:24
  155.0 3.1 %collective-permute-start.13 = (f32[8,32,1]{1,2,0:T(1,128)S(1)}, f32[8,32,1]{1,2,0:T(1,128)S(1)}, u32[]{:S(2)}, u32[]{:S(2)}) collective-permute-start(f32[8,32,1]{1,2,0:T(1,128)S(1)} %get-tuple-element.39), channel_id=1, source_target_pairs={{4,0},{8,4},{12,8},{16,12},{20,16},{24,20},{28,24},{5,1},{9,5},{13... | collective-permute-start | bytes 3080 | tf_op jit(solution)/shard_map/ppermute | solution.py:25
  158.3 10.3 %collective-permute-start.14 = (f32[8,1,66]{1,2,0:T(8,128)S(1)}, f32[8,1,66]{1,2,0:T(8,128)S(1)}, u32[]{:S(2)}, u32[]{:S(2)}) collective-permute-start(f32[8,1,66]{1,2,0:T(8,128)S(1)} %get-tuple-element.27), channel_id=1, source_target_pairs={{1,0},{2,1},{3,2},{5,4},{6,5},{7,6},{9,8},{10,9},{11,10},{13,12},{... | collective-permute-start | bytes 6344 | tf_op jit(solution)/shard_map/ppermute | solution.py:25
  159.6 10.7 %collective-permute-start.15 = (f32[8,1,66]{1,2,0:T(8,128)S(1)}, f32[8,1,66]{1,2,0:T(8,128)S(1)}, u32[]{:S(2)}, u32[]{:S(2)}) collective-permute-start(f32[8,1,66]{1,2,0:T(8,128)S(1)} %get-tuple-element.26), channel_id=1, source_target_pairs={{0,1},{1,2},{2,3},{4,5},{5,6},{6,7},{8,9},{9,10},{10,11},{12,13},{... | collective-permute-start | bytes 6344 | tf_op jit(solution)/shard_map/ppermute | solution.py:24
  171.1 4.8 %collective-permute-start.16 = (f32[8,32,1]{1,2,0:T(1,128)S(1)}, f32[8,32,1]{1,2,0:T(1,128)S(1)}, u32[]{:S(2)}, u32[]{:S(2)}) collective-permute-start(f32[8,32,1]{1,2,0:T(1,128)S(1)} %get-tuple-element.36), channel_id=1, source_target_pairs={{0,4},{4,8},{8,12},{12,16},{16,20},{20,24},{24,28},{1,5},{5,9},{9,... | collective-permute-start | bytes 3080 | tf_op jit(solution)/shard_map/ppermute | solution.py:24
  174.6 3.1 %collective-permute-start.17 = (f32[8,32,1]{1,2,0:T(1,128)S(1)}, f32[8,32,1]{1,2,0:T(1,128)S(1)}, u32[]{:S(2)}, u32[]{:S(2)}) collective-permute-start(f32[8,32,1]{1,2,0:T(1,128)S(1)} %get-tuple-element.37), channel_id=1, source_target_pairs={{4,0},{8,4},{12,8},{16,12},{20,16},{24,20},{28,24},{5,1},{9,5},{13... | collective-permute-start | bytes 3080 | tf_op jit(solution)/shard_map/ppermute | solution.py:25
  177.9 10.4 %collective-permute-start.18 = (f32[8,1,66]{1,2,0:T(8,128)S(1)}, f32[8,1,66]{1,2,0:T(8,128)S(1)}, u32[]{:S(2)}, u32[]{:S(2)}) collective-permute-start(f32[8,1,66]{1,2,0:T(8,128)S(1)} %get-tuple-element.25), channel_id=1, source_target_pairs={{1,0},{2,1},{3,2},{5,4},{6,5},{7,6},{9,8},{10,9},{11,10},{13,12},{... | collective-permute-start | bytes 6344 | tf_op jit(solution)/shard_map/ppermute | solution.py:25
  179.2 10.9 %collective-permute-start.19 = (f32[8,1,66]{1,2,0:T(8,128)S(1)}, f32[8,1,66]{1,2,0:T(8,128)S(1)}, u32[]{:S(2)}, u32[]{:S(2)}) collective-permute-start(f32[8,1,66]{1,2,0:T(8,128)S(1)} %get-tuple-element.24), channel_id=1, source_target_pairs={{0,1},{1,2},{2,3},{4,5},{5,6},{6,7},{8,9},{9,10},{10,11},{12,13},{... | collective-permute-start | bytes 6344 | tf_op jit(solution)/shard_map/ppermute | solution.py:24
  190.8 4.8 %collective-permute-start.20 = (f32[8,32,1]{1,2,0:T(1,128)S(1)}, f32[8,32,1]{1,2,0:T(1,128)S(1)}, u32[]{:S(2)}, u32[]{:S(2)}) collective-permute-start(f32[8,32,1]{1,2,0:T(1,128)S(1)} %get-tuple-element.30), channel_id=1, source_target_pairs={{0,4},{4,8},{8,12},{12,16},{16,20},{20,24},{24,28},{1,5},{5,9},{9,... | collective-permute-start | bytes 3080 | tf_op jit(solution)/shard_map/ppermute | solution.py:24
  194.3 3.3 %collective-permute-start.21 = (f32[8,32,1]{1,2,0:T(1,128)S(1)}, f32[8,32,1]{1,2,0:T(1,128)S(1)}, u32[]{:S(2)}, u32[]{:S(2)}) collective-permute-start(f32[8,32,1]{1,2,0:T(1,128)S(1)} %get-tuple-element.31), channel_id=1, source_target_pairs={{4,0},{8,4},{12,8},{16,12},{20,16},{24,20},{28,24},{5,1},{9,5},{13... | collective-permute-start | bytes 3080 | tf_op jit(solution)/shard_map/ppermute | solution.py:25
  197.8 10.6 %collective-permute-start.22 = (f32[8,1,66]{1,2,0:T(8,128)S(1)}, f32[8,1,66]{1,2,0:T(8,128)S(1)}, u32[]{:S(2)}, u32[]{:S(2)}) collective-permute-start(f32[8,1,66]{1,2,0:T(8,128)S(1)} %get-tuple-element.23), channel_id=1, source_target_pairs={{1,0},{2,1},{3,2},{5,4},{6,5},{7,6},{9,8},{10,9},{11,10},{13,12},{... | collective-permute-start | bytes 6344 | tf_op jit(solution)/shard_map/ppermute | solution.py:25
  199.1 11.0 %collective-permute-start.23 = (f32[8,1,66]{1,2,0:T(8,128)S(1)}, f32[8,1,66]{1,2,0:T(8,128)S(1)}, u32[]{:S(2)}, u32[]{:S(2)}) collective-permute-start(f32[8,1,66]{1,2,0:T(8,128)S(1)} %get-tuple-element.22), channel_id=1, source_target_pairs={{0,1},{1,2},{2,3},{4,5},{5,6},{6,7},{8,9},{9,10},{10,11},{12,13},{... | collective-permute-start | bytes 6344 | tf_op jit(solution)/shard_map/ppermute | solution.py:24
  229.5 28.2 %copy-start.4 = (bf16[8,4,8,128]{3,2,1,0:T(8,128)(2,1)S(1)}, bf16[8,4,8,128]{3,2,1,0:T(8,128)(2,1)}, u32[]{:S(2)}) copy-start(bf16[8,4,8,128]{3,2,1,0:T(8,128)(2,1)} %param.8) | copy-start | bytes 196612
  (6 other events, 21.0 us)
Sparse Core Ops, SparseCore 0:
  73.4 33.2 reduce-scatter.6
  233.1 24.5 reduce-scatter.4
